TPU v7x, 256 devices: a whole 4x4x8 slice. The times are simulated.
256 devices in a mesh: dp: 64 (over x, z, core), rep: 4 (over y).
Axes of the slice: x: 4, y: 4, z: 8, core: 2. Of those that a mesh axis runs over, the one named last changes fastest.
Arguments:
- frames_in: bfloat16 [4, 57344, 1536], P('rep', 'dp')
- lengths: int32 [4, 64, 4], P('rep', 'dp'), may hold values from 1 to 893, as said below
- norm_gain: float32 [1536], replicated, may hold values from 0.5 to 1.5
- norm_bias: float32 [1536], replicated, may hold values from -2 to 2
- w_in: bfloat16 [1536, 3072], P(('dp', 'rep')), may hold values from -0.15625 to 0.15625
- kernel: float32 [31, 1536], replicated, may hold values from -1 to 1
- batch_gain: float32 [1536], replicated, may hold values from 0.5 to 1.5
- batch_bias: float32 [1536], replicated, may hold values from -3 to 3
- w_out: bfloat16 [1536, 1536], P(('dp', 'rep')), may hold values from -0.15625 to 0.15625
Outputs:
- frames_out: bfloat16 [4, 57344, 1536], P('rep', 'dp')
Inputs may be any that keep to these rules, and one draw needn't show every extreme that they name: `lengths`: for each rep index, the devices 2k and 2k + 1 of dp hold 1024 frames together, so each rep index holds 512 frames for each of its dp devices; a device holds at most 896 frames, and some device of every rep index holds exactly 896.
All inputs are finite; a program needn't handle non-finite values.
Results may differ from a plain program's by a relative error of at most 0.0038.
Values may be sent and summed in bfloat16 or wider, within the bound.
A program may use at most 128 MiB of HBM per device.

v0:
```python
import jax
import jax.numpy as jnp
from jax import lax
from jax.sharding import PartitionSpec as P

FR_DEV = 512
EPSILON = 1e-05


def layer_norm(frames, norm_gain, norm_bias):
    values = frames.astype(jnp.float32)
    average = jnp.mean(values, axis=-1, keepdims=True)
    centred = values - average
    spread = jnp.mean(centred * centred, axis=-1, keepdims=True)
    return centred * lax.rsqrt(spread + EPSILON) * norm_gain + norm_bias


def depthwise(gated, labels, kernel):
    half_kernel = kernel.shape[0] // 2
    length_rows = gated.shape[0]
    padded = jnp.pad(gated, ((half_kernel, half_kernel), (0, 0)))
    padded_labels = jnp.pad(labels, (half_kernel, half_kernel), constant_values=-1)
    summed = jnp.zeros(gated.shape, jnp.float32)
    for offset in range(kernel.shape[0]):
        shared = padded_labels[offset : offset + length_rows] == labels
        contribution = jnp.where(
            shared[:, None], padded[offset : offset + length_rows].astype(jnp.float32), 0.0
        )
        summed = summed + contribution * kernel[offset]
    return summed


def project_in(normed, weight_rows):
    return jnp.dot(normed, weight_rows, preferred_element_type=jnp.float32)


def project_out(active, weight_rows):
    return jnp.dot(active, weight_rows, preferred_element_type=jnp.float32)


def on_device(
    frames_in, lengths, norm_gain, norm_bias, w_in, kernel, batch_gain, batch_bias, w_out
):
    local_frames = frames_in[0]
    local_lengths = lengths[0, 0]
    capacity = local_frames.shape[0]
    features = local_frames.shape[1]
    total_count = lax.axis_size("dp") * lax.axis_size("rep") * FR_DEV
    grouped = (w_in, w_out)
    grouped = (
        lax.all_gather(w_in, ("dp", "rep"), axis=0, tiled=True),
        lax.all_gather(w_out, ("dp", "rep"), axis=0, tiled=True),
    )
    rows_here = jnp.arange(capacity, dtype=jnp.int32)
    local_load = jnp.sum(local_lengths)
    bounds = jnp.cumsum(local_lengths)
    labels = jnp.sum((rows_here[:, None] >= bounds[None, :]).astype(jnp.int32), axis=1)
    row_weight = (rows_here < local_load).astype(jnp.float32)[:, None]
    normed = layer_norm(local_frames, norm_gain, norm_bias).astype(jnp.bfloat16)
    projected = project_in(normed, grouped[0])
    gated = (projected[:, :features] * jax.nn.sigmoid(projected[:, features:])).astype(jnp.bfloat16)
    convolved = depthwise(gated, labels, kernel)
    average = lax.psum(jnp.sum(convolved * row_weight, axis=0), ("dp", "rep")) / total_count
    centred = convolved - average
    spread = lax.psum(jnp.sum(centred * centred * row_weight, axis=0), ("dp", "rep")) / total_count
    scaled = centred * lax.rsqrt(spread + EPSILON) * batch_gain + batch_bias
    active = jax.nn.silu(scaled).astype(jnp.bfloat16)
    branch = project_out(active, grouped[1])
    mixed = (local_frames.astype(jnp.float32) + branch).astype(jnp.bfloat16)
    result = jnp.where(rows_here[:, None] < local_load, mixed, jnp.zeros_like(mixed))
    return result[None]


def solution(mesh):
    placed = (
        P("rep", "dp", None),
        P("rep", "dp", None),
        P(),
        P(),
        P(("dp", "rep"), None),
        P(),
        P(),
        P(),
        P(("dp", "rep"), None),
    )
    return jax.shard_map(
        on_device, mesh=mesh, in_specs=placed, out_specs=P("rep", "dp", None), check_vma=False
    )
```

profile of v0, /device:TPU:1, one launch (start us, length us, event | category | flops | bytes accessed | tf_op | source)
XLA Modules:
  0.0 487.7 jit_solution(4124133330554323458)
XLA Ops:
  6.5 0.0 all-gather.7.cloned.1.call-start
  6.5 0.7 all-gather.7.cloned.1.call-update
  7.3 0.0 all-gather.5.cloned.1.call-start
  7.3 0.7 all-gather.5.cloned.1.call-update
  8.0 1.3 reduce_sum.54
  9.3 0.8 reduce-window.8
  10.1 0.6 iota_compare_fusion.1
  10.8 0.7 fusion.26
  11.4 0.1 convert_reduce_fusion.1
  11.5 1.5 slice_reduce_fusion.29
  13.0 1.8 slice_reduce_fusion.30
  14.9 0.1 slice_compare_fusion.26
  14.9 2.2 convert_reduce_fusion
  17.2 2.6 fusion.4
  19.8 0.1 slice_compare_fusion.29
  19.9 0.1 slice_compare_fusion.28
  20.0 0.1 slice_compare_fusion.27
  20.1 111.2 %all-gather.7.cloned.1.call-done = bf16[256,6,1536]{2,1,0:T(8,128)(2,1)} async-done(((bf16[1,6,1536]{2,1,0:T(8,128)(2,1)}), bf16[256,6,1536]{2,1,0:T(8,128)(2,1)}) %all-gather.7.cloned.1.call-update) | async-done | bytes 4718608 | tf_op jit(solution)/shard_map/all_gather | solution.py:52
  131.3 8.5 %reshape.87 = bf16[1536,1536]{1,0:T(8,128)(2,1)} reshape(bf16[256,6,1536]{2,1,0:T(8,128)(2,1)} %all-gather.7.cloned.1.call-done) | data formatting | bytes 9437184
  139.8 0.0 copy-start
  139.8 0.0 copy-start.2
  139.8 0.0 copy-start.3
  139.8 113.5 %all-gather.5.cloned.1.call-done = bf16[256,6,3072]{2,1,0:T(8,128)(2,1)} async-done(((bf16[1,6,3072]{2,1,0:T(8,128)(2,1)}), bf16[256,6,3072]{2,1,0:T(8,128)(2,1)}) %all-gather.5.cloned.1.call-update) | async-done | bytes 9437200 | tf_op jit(solution)/shard_map/all_gather | solution.py:51
  253.3 14.2 %reshape.85 = bf16[1536,3072]{1,0:T(8,128)(2,1)} reshape(bf16[256,6,3072]{2,1,0:T(8,128)(2,1)} %all-gather.5.cloned.1.call-done) | data formatting | bytes 18874368
  267.5 0.0 copy-done
  267.5 0.0 copy-done.2
  267.5 0.0 copy-done.3
  267.5 11.3 %fusion.16 = f32[896,3072]{1,0:T(8,128)S(1)} fusion(bf16[1536,3072]{1,0:T(8,128)(2,1)} %reshape.85, bf16[1,896,1536]{2,1,0:T(8,128)(2,1)S(1)} %copy-done, f32[1536]{0:T(1024)S(1)} %copy-done.2, f32[1536]{0:T(1024)S(1)} %copy-done.3, f32[896]{0:T(1024)S(1)} %add_rsqrt_fusion.1, f32[896]{0:T(1024)S(1)} %broadcast_multiply_fusion.1), kind=kOutput, calls=%fused_computation.23 | convolution fusion | flops 8463974400 | bytes 23219200 | tf_op jit(solution)/shard_map/dot_general | solution.py:34
  278.8 1.5 fusion.13
  280.4 0.0 copy-start.4
  280.4 0.0 copy-start.5
  280.4 38.3 %multiply_reduce_fusion.1 = (f32[1536]{0:T(1024)S(1)}, f32[896,1536]{1,0:T(8,128)}) fusion(f32[896]{0:T(1024)S(1)} %fusion.26, f32[1536]{0:T(1024)S(1)} %get-tuple-element.34, pred[896]{0:T(1024)(128)(4,1)S(1)} %get-tuple-element.67, f32[1536]{0:T(1024)S(1)} %get-tuple-element.35, pred[896]{0:T(1024)(128)(4,1)S(1)} %get-tuple-element.39, ...), kind=kLoop, calls=%fused_computation.18 | loop fusion | flops 170654208 | bytes 8484608 | tf_op jit(solution)/shard_map/reduce_sum | solution.py:63
  318.7 0.0 copy-start.1
  318.7 74.8 %psum.14 = f32[1536]{0:T(1024)S(1)} all-reduce(f32[1536]{0:T(1024)S(1)} %get-tuple-element.36), channel_id=1, replica_groups=mesh['dp'=64,'rep'=4] {'dp','rep'}, use_global_device_ids=true, to_apply=%region_6.7 | all-reduce | flops 1536 | bytes 12288 | tf_op jit(solution)/shard_map/psum | solution.py:63
  393.5 3.3 multiply_reduce_fusion
  396.8 73.6 %psum.15 = f32[1536]{0:T(1024)S(1)} all-reduce(f32[1536]{0:T(1024)S(1)} %multiply_reduce_fusion), channel_id=1, replica_groups=mesh['dp'=64,'rep'=4] {'dp','rep'}, use_global_device_ids=true, to_apply=%region_8.9 | all-reduce | flops 1536 | bytes 12288 | tf_op jit(solution)/shard_map/psum | solution.py:65
  470.4 0.0 copy-done.4
  470.4 0.0 copy-done.5
  470.4 0.0 copy-done.1
  470.4 10.4 %fusion.15 = bf16[1,896,1536]{2,1,0:T(8,128)(2,1)} fusion(bf16[1536,1536]{1,0:T(8,128)(2,1)} %reshape.87, bf16[1,896,1536]{2,1,0:T(8,128)(2,1)S(1)} %copy-done.1, f32[896,1536]{1,0:T(8,128)} %get-tuple-element.37, f32[1536]{0:T(1024)S(1)} %copy-done.4, f32[1536]{0:T(1024)S(1)} %copy-done.5, f32[1536]{0:T(1024)S(1)} %add_rsqrt_fusion, ...), kind=kOutput, calls=%fused_computation.22 | convolution fusion | flops 4245749760 | bytes 15754112 | tf_op jit(solution)/shard_map/dot_general | solution.py:38
  (4 shorter events, 0.0 us)
Async XLA Ops:
  6.5 124.8 %all-gather.7.cloned.1.call-start = ((), (), s32[]{:S(2)}) async-start(), calls=%async_computation.1 | async-start | bytes 6316032 | tf_op jit(solution)/shard_map/all_gather | solution.py:52
  7.3 246.1 %all-gather.5.cloned.1.call-start = ((), (), s32[]{:S(2)}) async-start(), calls=%async_computation | async-start | bytes 12632064 | tf_op jit(solution)/shard_map/all_gather | solution.py:51
  139.8 127.7 %copy-start = (bf16[1,896,1536]{2,1,0:T(8,128)(2,1)S(1)}, bf16[1,896,1536]{2,1,0:T(8,128)(2,1)}, u32[]{:S(2)}) copy-start(bf16[1,896,1536]{2,1,0:T(8,128)(2,1)} %param.9) | copy-start | bytes 8257540
  139.8 127.7 %copy-start.2 = (f32[1536]{0:T(1024)S(1)}, f32[1536]{0:T(1024)}, u32[]{:S(2)}) copy-start(f32[1536]{0:T(1024)} %param.12) | copy-start | bytes 18436
  139.8 127.7 %copy-start.3 = (f32[1536]{0:T(1024)S(1)}, f32[1536]{0:T(1024)}, u32[]{:S(2)}) copy-start(f32[1536]{0:T(1024)} %param.11) | copy-start | bytes 18436
  280.4 190.1 %copy-start.4 = (f32[1536]{0:T(1024)S(1)}, f32[1536]{0:T(1024)}, u32[]{:S(2)}) copy-start(f32[1536]{0:T(1024)} %param.16) | copy-start | bytes 18436
  280.4 190.1 %copy-start.5 = (f32[1536]{0:T(1024)S(1)}, f32[1536]{0:T(1024)}, u32[]{:S(2)}) copy-start(f32[1536]{0:T(1024)} %param.15) | copy-start | bytes 18436
  318.7 151.7 %copy-start.1 = (bf16[1,896,1536]{2,1,0:T(8,128)(2,1)S(1)}, bf16[1,896,1536]{2,1,0:T(8,128)(2,1)}, u32[]{:S(2)}) copy-start(bf16[1,896,1536]{2,1,0:T(8,128)(2,1)} %param.9) | copy-start | bytes 8257540
Sparse Core Ops, SparseCore 0:
  11.2 120.0 all-gather.6
  135.1 118.1 all-gather.4
where the time goes:
time: 489 us; the launch traced here: 488 us
  waiting for transfers between devices  226 us (46%)
  blocking collectives  148 us (30%)
  other arithmetic  51.8 us (11%)
  local copies, waits for them, and re-layouts  26 us (5%)
  matrix products  21.8 us (4%)
  between operations  13.5 us (3%)
    all_gather x1, waiting for transfers between devices, on_device(): lax.all_gather(w_in, ('dp', 'rep'), axis=0, tiled=True)  114 us
    all_gather x1, waiting for transfers between devices, on_device(): lax.all_gather(w_out, ('dp', 'rep'), axis=0, tiled=True)  111 us
    psum x1, blocking collectives, on_device(): lax.psum(jnp.sum(convolved * row_weight, axis=0), ('dp', 'rep'))  74.8 us
    psum x1, blocking collectives, on_device(): lax.psum(jnp.sum(centred * centred * row_weight, axis=0), ('dp', 'rep'))  73.6 us
    reduce_sum x1, other arithmetic, on_device(): jnp.sum(convolved * row_weight, axis=0)  38.3 us
    unnamed x14, local copies, waits for them, and re-layouts  22.6 us
    dot_general x1, matrix products, project_in(): return jnp.dot(normed, weight_rows, preferred_element_type=jnp.float32)  11.3 us
    dot_general x1, matrix products, project_out(): return jnp.dot(active, weight_rows, preferred_element_type=jnp.float32)  10.4 us
  transfers between devices with their start and end apart: 2, of which 2 were waited for; matrix products, arithmetic and copies ran while one was open for 4% of the time, Pallas kernels for 0%

commit v1 on v0

--- a/solution.py
+++ b/solution.py
@@ -60,7 +60,7 @@
     projected = project_in(normed, grouped[0])
     gated = (projected[:, :features] * jax.nn.sigmoid(projected[:, features:])).astype(jnp.bfloat16)
     convolved = depthwise(gated, labels, kernel)
-    average = lax.psum(jnp.sum(convolved * row_weight, axis=0), ("dp", "rep")) / total_count
+    average = lax.psum(lax.psum(jnp.sum(convolved * row_weight, axis=0), "rep"), "dp") / total_count
     centred = convolved - average
     spread = lax.psum(jnp.sum(centred * centred * row_weight, axis=0), ("dp", "rep")) / total_count
     scaled = centred * lax.rsqrt(spread + EPSILON) * batch_gain + batch_bias

time: 489 us -> 550 us (1.12)
  blocking collectives: 148 us -> 209 us
    psum x1 -> x2, blocking collectives: 74.8 us -> 136 us  [the longest x1 128 us: on_device(): lax.psum(lax.psum(jnp.sum(convolved * row_weight, axis=0), 'rep'), 'dp')]
where the time goes in v1:
time: 550 us; the launch traced here: 549 us
  waiting for transfers between devices  226 us (41%)
  blocking collectives  209 us (38%)
  other arithmetic  51.8 us (9%)
  local copies, waits for them, and re-layouts  26 us (5%)
  matrix products  21.8 us (4%)
  between operations  13.5 us (2%)
    psum x1, blocking collectives, on_device(): lax.psum(lax.psum(jnp.sum(convolved * row_weight, axis=0), 'rep'), 'dp')  128 us
    all_gather x1, waiting for transfers between devices, on_device(): lax.all_gather(w_in, ('dp', 'rep'), axis=0, tiled=True)  114 us
    all_gather x1, waiting for transfers between devices, on_device(): lax.all_gather(w_out, ('dp', 'rep'), axis=0, tiled=True)  111 us
    psum x1, blocking collectives, on_device(): lax.psum(jnp.sum(centred * centred * row_weight, axis=0), ('dp', 'rep'))  72.7 us
    reduce_sum x1, other arithmetic, on_device(): jnp.sum(convolved * row_weight, axis=0)  38.3 us
    unnamed x14, local copies, waits for them, and re-layouts  22.6 us
    dot_general x1, matrix products, project_in(): return jnp.dot(normed, weight_rows, preferred_element_type=jnp.float32)  11.3 us
  transfers between devices with their start and end apart: 2, of which 2 were waited for; matrix products, arithmetic and copies ran while one was open for 4% of the time, Pallas kernels for 0%

profile of v1, /device:TPU:1, one launch (start us, length us, event | category | flops | bytes accessed | tf_op | source)
XLA Modules:
  0.0 548.5 jit_solution(2764939833308996390)
XLA Ops:
  6.5 0.0 all-gather.7.cloned.1.call-start
  6.5 0.7 all-gather.7.cloned.1.call-update
  7.3 0.0 all-gather.5.cloned.1.call-start
  7.3 0.7 all-gather.5.cloned.1.call-update
  8.0 1.3 reduce_sum.54
  9.3 0.8 reduce-window.8
  10.1 0.6 iota_compare_fusion.1
  10.8 0.7 fusion.26
  11.4 0.1 convert_reduce_fusion.1
  11.5 1.5 slice_reduce_fusion.29
  13.0 1.8 slice_reduce_fusion.30
  14.9 0.1 slice_compare_fusion.26
  14.9 2.2 convert_reduce_fusion
  17.2 2.6 fusion.4
  19.8 0.1 slice_compare_fusion.29
  19.9 0.1 slice_compare_fusion.28
  20.0 0.1 slice_compare_fusion.27
  20.1 111.2 %all-gather.7.cloned.1.call-done = bf16[256,6,1536]{2,1,0:T(8,128)(2,1)} async-done(((bf16[1,6,1536]{2,1,0:T(8,128)(2,1)}), bf16[256,6,1536]{2,1,0:T(8,128)(2,1)}) %all-gather.7.cloned.1.call-update) | async-done | bytes 4718608 | tf_op jit(solution)/shard_map/all_gather | solution.py:52
  131.3 8.5 %reshape.87 = bf16[1536,1536]{1,0:T(8,128)(2,1)} reshape(bf16[256,6,1536]{2,1,0:T(8,128)(2,1)} %all-gather.7.cloned.1.call-done) | data formatting | bytes 9437184
  139.8 0.0 copy-start
  139.8 0.0 copy-start.2
  139.8 0.0 copy-start.3
  139.8 113.5 %all-gather.5.cloned.1.call-done = bf16[256,6,3072]{2,1,0:T(8,128)(2,1)} async-done(((bf16[1,6,3072]{2,1,0:T(8,128)(2,1)}), bf16[256,6,3072]{2,1,0:T(8,128)(2,1)}) %all-gather.5.cloned.1.call-update) | async-done | bytes 9437200 | tf_op jit(solution)/shard_map/all_gather | solution.py:51
  253.3 14.2 %reshape.85 = bf16[1536,3072]{1,0:T(8,128)(2,1)} reshape(bf16[256,6,3072]{2,1,0:T(8,128)(2,1)} %all-gather.5.cloned.1.call-done) | data formatting | bytes 18874368
  267.5 0.0 copy-done
  267.5 0.0 copy-done.2
  267.5 0.0 copy-done.3
  267.5 11.3 %fusion.16 = f32[896,3072]{1,0:T(8,128)S(1)} fusion(bf16[1536,3072]{1,0:T(8,128)(2,1)} %reshape.85, bf16[1,896,1536]{2,1,0:T(8,128)(2,1)S(1)} %copy-done, f32[1536]{0:T(1024)S(1)} %copy-done.2, f32[1536]{0:T(1024)S(1)} %copy-done.3, f32[896]{0:T(1024)S(1)} %add_rsqrt_fusion.1, f32[896]{0:T(1024)S(1)} %broadcast_multiply_fusion.1), kind=kOutput, calls=%fused_computation.23 | convolution fusion | flops 8463974400 | bytes 23219200 | tf_op jit(solution)/shard_map/dot_general | solution.py:34
  278.8 1.5 fusion.13
  280.4 0.0 copy-start.4
  280.4 0.0 copy-start.5
  280.4 38.3 %multiply_reduce_fusion.1 = (f32[1536]{0:T(1024)S(1)}, f32[896,1536]{1,0:T(8,128)}) fusion(f32[896]{0:T(1024)S(1)} %fusion.26, f32[1536]{0:T(1024)S(1)} %get-tuple-element.34, pred[896]{0:T(1024)(128)(4,1)S(1)} %get-tuple-element.67, f32[1536]{0:T(1024)S(1)} %get-tuple-element.35, pred[896]{0:T(1024)(128)(4,1)S(1)} %get-tuple-element.39, ...), kind=kLoop, calls=%fused_computation.18 | loop fusion | flops 170654208 | bytes 8484608 | tf_op jit(solution)/shard_map/reduce_sum | solution.py:63
  318.7 0.0 copy-start.1
  318.7 8.8 %psum.21 = f32[1536]{0:T(1024)S(1)} all-reduce(f32[1536]{0:T(1024)S(1)} %get-tuple-element.36), channel_id=1, replica_groups=mesh['dp'=64,'rep'=4] {'rep'}, use_global_device_ids=true, to_apply=%region_6.7 | all-reduce | flops 1536 | bytes 12288 | tf_op jit(solution)/shard_map/psum | solution.py:63
  327.5 127.7 %psum.22 = f32[1536]{0:T(1024)S(1)} all-reduce(f32[1536]{0:T(1024)S(1)} %psum.21), channel_id=1, replica_groups=mesh['dp'=64,'rep'=4] {'dp'}, use_global_device_ids=true, to_apply=%region_7.8 | all-reduce | flops 1536 | bytes 12288 | tf_op jit(solution)/shard_map/psum | solution.py:63
  455.2 3.3 multiply_reduce_fusion
  458.5 72.7 %psum.23 = f32[1536]{0:T(1024)S(1)} all-reduce(f32[1536]{0:T(1024)S(1)} %multiply_reduce_fusion), channel_id=1, replica_groups=mesh['dp'=64,'rep'=4] {'dp','rep'}, use_global_device_ids=true, to_apply=%region_9.10 | all-reduce | flops 1536 | bytes 12288 | tf_op jit(solution)/shard_map/psum | solution.py:65
  531.2 0.0 copy-done.4
  531.2 0.0 copy-done.5
  531.2 0.0 copy-done.1
  531.2 10.5 %fusion.15 = bf16[1,896,1536]{2,1,0:T(8,128)(2,1)} fusion(bf16[1536,1536]{1,0:T(8,128)(2,1)} %reshape.87, bf16[1,896,1536]{2,1,0:T(8,128)(2,1)S(1)} %copy-done.1, f32[896,1536]{1,0:T(8,128)} %get-tuple-element.37, f32[1536]{0:T(1024)S(1)} %copy-done.4, f32[1536]{0:T(1024)S(1)} %copy-done.5, f32[1536]{0:T(1024)S(1)} %add_rsqrt_fusion, ...), kind=kOutput, calls=%fused_computation.22 | convolution fusion | flops 4245749760 | bytes 15754112 | tf_op jit(solution)/shard_map/dot_general | solution.py:38
  (4 shorter events, 0.0 us)
Async XLA Ops:
  6.5 124.8 %all-gather.7.cloned.1.call-start = ((), (), s32[]{:S(2)}) async-start(), calls=%async_computation.1 | async-start | bytes 6316032 | tf_op jit(solution)/shard_map/all_gather | solution.py:52
  7.3 246.1 %all-gather.5.cloned.1.call-start = ((), (), s32[]{:S(2)}) async-start(), calls=%async_computation | async-start | bytes 12632064 | tf_op jit(solution)/shard_map/all_gather | solution.py:51
  139.8 127.7 %copy-start = (bf16[1,896,1536]{2,1,0:T(8,128)(2,1)S(1)}, bf16[1,896,1536]{2,1,0:T(8,128)(2,1)}, u32[]{:S(2)}) copy-start(bf16[1,896,1536]{2,1,0:T(8,128)(2,1)} %param.9) | copy-start | bytes 8257540
  139.8 127.7 %copy-start.2 = (f32[1536]{0:T(1024)S(1)}, f32[1536]{0:T(1024)}, u32[]{:S(2)}) copy-start(f32[1536]{0:T(1024)} %param.12) | copy-start | bytes 18436
  139.8 127.7 %copy-start.3 = (f32[1536]{0:T(1024)S(1)}, f32[1536]{0:T(1024)}, u32[]{:S(2)}) copy-start(f32[1536]{0:T(1024)} %param.11) | copy-start | bytes 18436
  280.4 250.9 %copy-start.4 = (f32[1536]{0:T(1024)S(1)}, f32[1536]{0:T(1024)}, u32[]{:S(2)}) copy-start(f32[1536]{0:T(1024)} %param.16) | copy-start | bytes 18436
  280.4 250.8 %copy-start.5 = (f32[1536]{0:T(1024)S(1)}, f32[1536]{0:T(1024)}, u32[]{:S(2)}) copy-start(f32[1536]{0:T(1024)} %param.15) | copy-start | bytes 18436
  318.7 212.5 %copy-start.1 = (bf16[1,896,1536]{2,1,0:T(8,128)(2,1)S(1)}, bf16[1,896,1536]{2,1,0:T(8,128)(2,1)}, u32[]{:S(2)}) copy-start(bf16[1,896,1536]{2,1,0:T(8,128)(2,1)} %param.9) | copy-start | bytes 8257540
Sparse Core Ops, SparseCore 0:
  11.2 120.0 all-gather.6
  135.1 118.1 all-gather.4
